TPU v7x, 32 devices: a whole 2x2x4 slice. The times are simulated.
32 devices in a mesh: row: 4 (over x, core), col: 8 (over z, y).
Axes of the slice: x: 2, y: 2, z: 4, core: 2. Of those that a mesh axis runs over, the one named last changes fastest.
Arguments:
- adj_trailing: bfloat16 [4096, 8192], P('row', 'col'), may hold values from -6 to 6
- panel_rows0: bfloat16 [4096, 512], P('row'), may hold values from -0.09375 to 0.09375
- panel_rows1: bfloat16 [4096, 512], P('row'), may hold values from -0.09375 to 0.09375
- panel_cols0: bfloat16 [8192, 512], P('col'), may hold values from -0.0625 to 0.0625
- panel_cols1: bfloat16 [8192, 512], P('col'), may hold values from -0.0625 to 0.0625
- inv_diag0: float32 [512, 512], replicated, as said below
- inv_diag1: float32 [512, 512], replicated, as said below
- cross_block: float32 [512, 512], replicated, may hold values from -0.25 to 0.25
- panel_adj0: bfloat16 [4096, 512], P(('row', 'col')), may hold values from -6 to 6
- panel_adj1: bfloat16 [4096, 512], P(('row', 'col')), may hold values from -6 to 6
Outputs:
- row_adj1: float32 [4096, 512], P(('row', 'col'))
- row_adj0: float32 [4096, 512], P(('row', 'col'))
- col_adj1: float32 [8192, 512], P('col')
- col_adj0: float32 [8192, 512], P('col')
- diag_adj1: float32 [512, 512], replicated
- diag_adj0: float32 [512, 512], replicated
Inputs may be any that keep to these rules, and one draw needn't show every extreme that they name: `inv_diag0`: lower triangular, with diagonal entries of 1 to 2. `inv_diag1`: lower triangular, with diagonal entries of 1 to 2.
All inputs are finite; a program needn't handle non-finite values.
Results may differ from a plain program's by a relative error of at most 0.0003.
Values sent between devices are 32-bit elements; how exact they have to be, the bound alone decides.
No kernel may reach another device: no remote copies, remote signals or barrier semaphores. Data moves between devices by JAX's collectives and lax.ppermute only.
A program may use at most 128 MiB of HBM per device.

v0:
```python
import jax
import jax.numpy as jnp
from jax import lax
from jax.sharding import PartitionSpec as P


def trailing_term(adj_trailing, columns):
    return jnp.dot(adj_trailing, columns, preferred_element_type=jnp.float32)


def column_term(adj_trailing, rows):
    return -jnp.einsum("rc,rb->cb", adj_trailing, rows, preferred_element_type=jnp.float32)


def local(
    adj_trailing,
    panel_rows0,
    panel_rows1,
    panel_cols0,
    panel_cols1,
    inv_diag0,
    inv_diag1,
    cross_block,
    panel_adj0,
    panel_adj1,
):
    highest = lax.Precision.HIGHEST
    share = panel_adj1.shape[0]
    width = panel_cols1.shape[1]
    offset = lax.axis_index("col") * share
    own_rows1 = lax.dynamic_slice_in_dim(panel_rows1, offset, share, 0).astype(jnp.float32)
    own_rows0 = lax.dynamic_slice_in_dim(panel_rows0, offset, share, 0).astype(jnp.float32)
    both_cols = jnp.concatenate((panel_cols1, panel_cols0), axis=1)
    trail = lax.psum_scatter(
        trailing_term(adj_trailing, both_cols), "col", scatter_dimension=0, tiled=True
    )
    trail1 = trail[:, :width]
    trail0 = trail[:, width:]
    both_rows = jnp.concatenate((panel_rows1, panel_rows0), axis=1)
    column_sum = lax.psum(column_term(adj_trailing, both_rows), "row")
    col_adj1 = column_sum[:, :width]
    col_adj0 = column_sum[:, width:]
    bar1 = panel_adj1.astype(jnp.float32) - trail1
    row_adj1 = jnp.dot(bar1, inv_diag1, precision=highest)
    bar0 = (
        panel_adj0.astype(jnp.float32) - trail0 - jnp.dot(row_adj1, cross_block, precision=highest)
    )
    row_adj0 = jnp.dot(bar0, inv_diag0, precision=highest)
    gram1 = jnp.dot(bar1.T, own_rows1, precision=highest)
    gram0 = jnp.dot(bar0.T, own_rows0, precision=highest)
    local1 = jnp.dot(inv_diag1.T, gram1, precision=highest)
    local0 = jnp.dot(inv_diag0.T, gram0, precision=highest)
    summed1, summed0 = lax.psum((local1, local0), ("row", "col"))
    diag_adj1 = -jnp.tril(summed1)
    diag_adj0 = -jnp.tril(summed0)
    return (row_adj1, row_adj0, col_adj1, col_adj0, diag_adj1, diag_adj0)


def solution(mesh):
    return jax.shard_map(
        local,
        mesh=mesh,
        in_specs=(
            P("row", "col"),
            P("row", None),
            P("row", None),
            P("col", None),
            P("col", None),
            P(),
            P(),
            P(),
            P(("row", "col"), None),
            P(("row", "col"), None),
        ),
        out_specs=(
            P(("row", "col"), None),
            P(("row", "col"), None),
            P("col", None),
            P("col", None),
            P(),
            P(),
        ),
        check_vma=False,
    )
```

profile of v0, /device:TPU:0, one launch (start us, length us, event | category | flops | bytes accessed | tf_op | source)
XLA Modules:
  0.0 268.3 jit_solution(9926880069097998248)
XLA Ops:
  8.0 0.0 copy-start
  8.0 0.0 reduce-scatter.2.cloned.1.call-start
  8.1 1.5 copy-done
  9.6 5.9 %convolution_bitcast_fusion = f32[1024,1024]{0,1:T(8,128)} fusion(bf16[1024,1024]{1,0:T(8,128)(2,1)S(1)} %copy-done, bf16[1024,512]{1,0:T(8,128)(2,1)} %param.13, bf16[1024,512]{1,0:T(8,128)(2,1)} %param.14), kind=kOutput, calls=%fused_computation.1 | convolution fusion | flops 2151677952 | bytes 8388608 | tf_op jit(solution)/shard_map/dot_general | solution.py:8
  15.5 0.0 copy-start.9
  15.5 0.0 reduce-scatter.2.cloned.1.call-update
  15.5 0.0 all-reduce.4.cloned.1.call-start
  15.6 1.1 copy-done.9
  16.7 5.6 %negate_bitcast_fusion = f32[1024,1024]{0,1:T(8,128)} fusion(bf16[1024,1024]{1,0:T(8,128)(2,1)S(1)} %copy-done, bf16[1024,512]{1,0:T(8,128)(2,1)} %param.11, bf16[1024,512]{1,0:T(8,128)(2,1)S(1)} %copy-done.9), kind=kOutput, calls=%fused_computation | convolution fusion | flops 2152726528 | bytes 8388608 | tf_op jit(solution)/shard_map/rc,rb->cb/dot_general | solution.py:12
  22.3 0.0 copy-start.7
  22.3 0.0 copy-start.8
  22.3 0.0 copy-start.2
  22.3 0.0 all-reduce.4.cloned.1.call-update
  22.3 0.2 all-reduce.6.cloned.1.call-start
  22.5 0.6 copy-done.7
  23.2 0.1 copy.16
  23.3 0.0 copy-done.8
  23.3 0.8 copy.17
  24.1 83.0 %reduce-scatter.2.cloned.1.call-done = f32[128,1024]{0,1:T(8,128)} async-done(((f32[1024,1024]{0,1:T(8,128)}), f32[128,1024]{0,1:T(8,128)}) %reduce-scatter.2.cloned.1.call-update) | async-done | bytes 524304 | tf_op jit(solution)/shard_map/reduce_scatter | solution.py:34
  107.1 0.0 copy-done.2
  107.1 0.0 copy-start.6
  107.1 1.8 fusion.7
  108.9 0.0 copy-done.6
  108.9 0.0 copy-start.5
  108.9 0.0 copy-start.4
  108.9 0.0 copy-start.3
  108.9 2.9 %convolution_subtract_fusion = f32[128,512]{0,1:T(8,128)S(1)} fusion(f32[128,512]{1,0:T(8,128)S(1)} %fusion.7, f32[512,512]{1,0:T(8,128)S(1)} %copy-done.6, f32[128,1024]{0,1:T(8,128)} %reduce-scatter.2.cloned.1.call-done, bf16[128,512]{0,1:T(8,128)(2,1)} %copy.17), kind=kOutput, calls=%fused_computation.10 | convolution fusion | flops 402849792 | bytes 1966080 | tf_op jit(solution)/shard_map/dot_general | solution.py:46
  111.8 0.0 copy-done.5
  111.8 1.5 fusion.8
  113.3 0.0 copy-done.4
  113.3 0.0 copy-start.1
  113.3 1.6 fusion.6
  114.9 0.0 copy-done.3
  114.9 2.8 %convolution_bitcast_fusion.2 = f32[512,512]{0,1:T(8,128)} fusion(f32[512,512]{1,0:T(8,128)S(1)} %fusion.6, f32[512,512]{1,0:T(8,128)S(1)} %copy-done.3), kind=kOutput, calls=%fused_computation.9 | convolution fusion | flops 1610612736 | bytes 3145728 | tf_op jit(solution)/shard_map/dot_general | solution.py:51
  117.8 0.0 copy-done.1
  117.8 2.8 %convolution_bitcast_fusion.1 = f32[512,512]{0,1:T(8,128)} fusion(f32[512,512]{1,0:T(8,128)S(1)} %fusion.8, f32[512,512]{1,0:T(8,128)S(1)} %copy-done.1), kind=kOutput, calls=%fused_computation.8 | convolution fusion | flops 1610612736 | bytes 3145728 | tf_op jit(solution)/shard_map/dot_general | solution.py:52
  120.6 0.0 all-reduce.6.cloned.1.call-update
  120.6 0.0 all-reduce.4.cloned.1.call-done
  120.6 4.8 %fusion.15 = (f32[1024,512]{0,1:T(8,128)}, f32[1024,512]{0,1:T(8,128)}) fusion(f32[1024,1024]{0,1:T(8,128)} %all-reduce.4.cloned.1.call-done), kind=kLoop, calls=%fused_computation.25 | loop fusion | bytes 8388608 | tf_op jit(solution)/shard_map/slice | solution.py:42
  125.5 2.9 %copy.19 = f32[1024,512]{1,0:T(8,128)} copy(f32[1024,512]{0,1:T(8,128)} %get-tuple-element.15) | data formatting | bytes 4194304
  128.4 2.9 %copy.20 = f32[1024,512]{1,0:T(8,128)} copy(f32[1024,512]{0,1:T(8,128)} %get-tuple-element.14) | data formatting | bytes 4194304
  131.3 1.5 fusion.16
  132.7 121.5 %all-reduce.6.cloned.1.call-done = (f32[512,512]{0,1:T(8,128)}, f32[512,512]{0,1:T(8,128)}) async-done(((f32[512,512]{0,1:T(8,128)}, f32[512,512]{0,1:T(8,128)}), (f32[512,512]{0,1:T(8,128)}, f32[512,512]{0,1:T(8,128)})) %all-reduce.6.cloned.1.call-update) | async-done | bytes 2097168 | tf_op jit(solution)/shard_map/psum | solution.py:53
  254.2 2.8 %select_negate_fusion = (f32[512,512]{0,1:T(8,128)S(1)}, f32[512,512]{0,1:T(8,128)}) fusion(f32[512,512]{0,1:T(8,128)} %get-tuple-element.13, f32[512,512]{0,1:T(8,128)} %get-tuple-element.12), kind=kLoop, calls=%fused_computation.11 | loop fusion | flops 1310720 | bytes 4194304 | tf_op jit(solution)/shard_map/neg | solution.py:55
  257.0 2.5 copy.21
  259.6 1.3 copy.22
Async XLA Ops:
  8.0 1.6 copy-start
  8.0 99.0 %reduce-scatter.2.cloned.1.call-start = ((), (), s32[]{:S(2)}) async-start(), calls=%async_computation.1 | async-start | bytes 4718592 | tf_op jit(solution)/shard_map/reduce_scatter | solution.py:34
  15.5 1.2 copy-start.9
  15.5 105.1 %all-reduce.4.cloned.1.call-start = ((), (), s32[]{:S(2)}) async-start(), calls=%async_computation.2 | async-start | bytes 8388608 | tf_op jit(solution)/shard_map/psum | solution.py:40
  22.3 0.9 copy-start.7
  22.3 1.0 copy-start.8
  22.3 84.8 %copy-start.2 = (f32[512,512]{1,0:T(8,128)S(1)}, f32[512,512]{1,0:T(8,128)}, u32[]{:S(2)}) copy-start(f32[512,512]{1,0:T(8,128)} %param.16) | copy-start | bytes 3145732
  22.3 231.9 %all-reduce.6.cloned.1.call-start = ((), (), s32[]{:S(2)}) async-start(), calls=%async_computation.3 | async-start | bytes 4194304 | tf_op jit(solution)/shard_map/psum | solution.py:53
  107.1 1.8 copy-start.6
  108.9 3.0 %copy-start.5 = (f32[128,512]{1,0:T(8,128)}, f32[128,512]{1,0:T(8,128)S(1)}, u32[]{:S(2)}) copy-start(f32[128,512]{1,0:T(8,128)S(1)} %fusion.7) | copy-start | bytes 786436
  108.9 4.4 %copy-start.4 = (f32[128,1024]{0,1:T(8,128)S(1)}, f32[128,1024]{0,1:T(8,128)}, u32[]{:S(2)}) copy-start(f32[128,1024]{0,1:T(8,128)} %reduce-scatter.2.cloned.1.call-done) | copy-start | bytes 1572868
  108.9 6.0 %copy-start.3 = (f32[512,512]{1,0:T(8,128)S(1)}, f32[512,512]{1,0:T(8,128)}, u32[]{:S(2)}) copy-start(f32[512,512]{1,0:T(8,128)} %param.16) | copy-start | bytes 3145732
  113.3 4.4 %copy-start.1 = (f32[512,512]{1,0:T(8,128)S(1)}, f32[512,512]{1,0:T(8,128)}, u32[]{:S(2)}) copy-start(f32[512,512]{1,0:T(8,128)} %param.15) | copy-start | bytes 3145732
Sparse Core Ops, SparseCore 0:
  15.6 91.3 reduce-scatter.1
Sparse Core Ops, SparseCore 1:
  22.4 88.0 all-reduce.3
  120.7 133.5 all-reduce.5
where the time goes:
time: 269 us; the launch traced here: 268 us
  waiting for transfers between devices  205 us (76%)
  matrix products  26.3 us (10%)
  local copies, waits for them, and re-layouts  18.7 us (7%)
  between operations  15.6 us (6%)
  other arithmetic  2.78 us (1%)
    psum x1, waiting for transfers between devices, local(): summed1, summed0 = lax.psum((local1, local0), ('row', 'col'))  122 us
    reduce_scatter x1, waiting for transfers between devices, local(): lax.psum_scatter(trailing_term(adj_trailing, both_cols), 'col', scatter_d...  83 us
    unnamed x26, local copies, waits for them, and re-layouts  13.9 us
    dot_general x1, matrix products, trailing_term(): return jnp.dot(adj_trailing, columns, preferred_element_type=jnp.float32)  5.88 us
    dot_general x1, matrix products, column_term(): jnp.einsum('rc,rb->cb', adj_trailing, rows, preferred_element_type=jnp.fl...  5.57 us
  transfers between devices with their start and end apart: 3, of which 2 were waited for; matrix products, arithmetic and copies ran while one was open for 12% of the time, Pallas kernels for 0%

commit v1 on v0

--- a/solution.py
+++ b/solution.py
@@ -50,7 +50,7 @@
     gram0 = jnp.dot(bar0.T, own_rows0, precision=highest)
     local1 = jnp.dot(inv_diag1.T, gram1, precision=highest)
     local0 = jnp.dot(inv_diag0.T, gram0, precision=highest)
-    summed1, summed0 = lax.psum((local1, local0), ("row", "col"))
+    summed1, summed0 = lax.psum(lax.psum((local1, local0), "col"), "row")
     diag_adj1 = -jnp.tril(summed1)
     diag_adj0 = -jnp.tril(summed0)
     return (row_adj1, row_adj0, col_adj1, col_adj0, diag_adj1, diag_adj0)

time: 269 us -> 365 us (1.36)
  waiting for transfers between devices: 205 us -> 306 us
    psum x1, waiting for transfers between devices: 0.03 us -> 120 us  [local(): column_sum = lax.psum(column_term(adj_trailing, both_rows), 'row')]
    psum x1, waiting for transfers between devices: 122 us -> 96 us  [local(): summed1, summed0 = lax.psum(lax.psum((local1, local0), 'col'), 'row')]
    reduce_scatter x1, waiting for transfers between devices: 83 us -> 89.5 us  [local(): lax.psum_scatter(trailing_term(adj_trailing, both_cols), 'col', scatter_d...]
    unnamed x26 -> x20, local copies, waits for them, and re-layouts: 13.9 us -> 13.1 us
  transfers between devices with their start and end apart: 3 -> 3, of which waited for: 2 -> 3; matrix products, arithmetic and copies ran while one was open for 12% -> 2% of each run, Pallas kernels for 0% -> 0%
where the time goes in v1:
time: 365 us
  waiting for transfers between devices  306 us (84%)
  matrix products  24.5 us (7%)
  local copies, waits for them, and re-layouts  18 us (5%)
  between operations  13.9 us (4%)
    psum x1, waiting for transfers between devices, local(): column_sum = lax.psum(column_term(adj_trailing, both_rows), 'row')  120 us
    psum x1, waiting for transfers between devices, local(): summed1, summed0 = lax.psum(lax.psum((local1, local0), 'col'), 'row')  96 us
    reduce_scatter x1, waiting for transfers between devices, local(): lax.psum_scatter(trailing_term(adj_trailing, both_cols), 'col', scatter_d...  89.5 us
    unnamed x20, local copies, waits for them, and re-layouts  13.1 us
  transfers between devices with their start and end apart: 3, of which 3 were waited for; matrix products, arithmetic and copies ran while one was open for 2% of the time, Pallas kernels for 0%

profile of v1, /device:TPU:0, one launch (start us, length us, event | category | flops | bytes accessed | tf_op | source)
XLA Modules:
  0.0 365.0 jit_solution(15254806995191913442)
XLA Ops:
  7.2 0.0 copy-start
  7.2 0.0 reduce-scatter.2.cloned.1.call-start
  7.2 1.5 copy-done
  8.8 5.9 %convolution_bitcast_fusion = f32[1024,1024]{0,1:T(8,128)} fusion(bf16[1024,1024]{1,0:T(8,128)(2,1)S(1)} %copy-done, bf16[1024,512]{1,0:T(8,128)(2,1)} %param.13, bf16[1024,512]{1,0:T(8,128)(2,1)} %param.14), kind=kOutput, calls=%fused_computation.1 | convolution fusion | flops 2151677952 | bytes 8388608 | tf_op jit(solution)/shard_map/dot_general | solution.py:8
  14.6 0.0 copy-start.6
  14.6 0.0 reduce-scatter.2.cloned.1.call-update
  14.7 0.0 copy-start.2
  14.7 0.0 all-reduce.5.cloned.1.call-start
  14.7 0.8 copy-done.6
  15.5 0.1 copy.16
  15.7 1.0 copy.17
  16.7 89.5 %reduce-scatter.2.cloned.1.call-done = f32[128,1024]{0,1:T(8,128)} async-done(((f32[1024,1024]{0,1:T(8,128)}), f32[128,1024]{0,1:T(8,128)}) %reduce-scatter.2.cloned.1.call-update) | async-done | bytes 524304 | tf_op jit(solution)/shard_map/reduce_scatter | solution.py:34
  106.2 0.0 copy-start.3
  106.2 1.6 fusion.6
  107.8 0.0 copy-done.2
  107.8 0.0 copy-start.5
  107.9 2.8 convolution_bitcast_fusion.2
  110.7 0.0 copy-done.3
  110.7 0.8 fusion.7
  111.5 0.0 copy-done.5
  111.5 0.0 copy-start.4
  111.5 0.0 copy-start.1
  111.5 1.8 convolution_subtract_fusion
  113.3 0.0 copy-done.4
  113.3 1.5 fusion.8
  114.8 0.0 copy-done.1
  114.8 2.8 convolution_bitcast_fusion.1
  117.6 0.0 all-reduce.5.cloned.1.call-update
  117.7 0.2 all-reduce.7.cloned.1.call-start
  117.9 5.9 %negate_bitcast_fusion = f32[1024,1024]{0,1:T(8,128)} fusion(bf16[1024,1024]{1,0:T(8,128)(2,1)S(1)} %copy-done, bf16[1024,512]{1,0:T(8,128)(2,1)} %param.11, bf16[1024,512]{1,0:T(8,128)(2,1)} %param.12), kind=kOutput, calls=%fused_computation | convolution fusion | flops 2152726528 | bytes 8388608 | tf_op jit(solution)/shard_map/rc,rb->cb/dot_general | solution.py:12
  123.8 96.0 %all-reduce.5.cloned.1.call-done = (f32[512,512]{0,1:T(8,128)}, f32[512,512]{0,1:T(8,128)}) async-done(((f32[512,512]{0,1:T(8,128)}, f32[512,512]{0,1:T(8,128)}), (f32[512,512]{0,1:T(8,128)}, f32[512,512]{0,1:T(8,128)})) %all-reduce.5.cloned.1.call-update) | async-done | bytes 2097168 | tf_op jit(solution)/shard_map/psum | solution.py:53
  219.8 0.0 all-reduce.7.cloned.1.call-update
  219.8 1.5 fusion.16
  221.3 120.0 %all-reduce.7.cloned.1.call-done = (f32[1024,1024]{0,1:T(8,128)}, f32[512,512]{0,1:T(8,128)}, f32[512,512]{0,1:T(8,128)}) async-done(((f32[1024,1024]{0,1:T(8,128)}, f32[512,512]{0,1:T(8,128)}, f32[512,512]{0,1:T(8,128)}), (f32[1024,1024]{0,1:T(8,128)}, f32[512,512]{0,1:T(8,128)}, f32[512,512]{0,1:T(8,128)})) %all-reduce.7.cloned.1.call-update) | async-done | bytes 6291472 | tf_op jit(solution)/shard_map/psum | solution.py:40
  341.2 4.8 %fusion.15 = (f32[1024,512]{0,1:T(8,128)}, f32[1024,512]{0,1:T(8,128)}) fusion(f32[1024,1024]{0,1:T(8,128)} %get-tuple-element.14), kind=kLoop, calls=%fused_computation.25 | loop fusion | bytes 8388608 | tf_op jit(solution)/shard_map/slice | solution.py:42
  346.1 2.9 copy.20
  348.9 2.9 copy.19
  351.8 2.8 select_negate_fusion
  354.6 2.5 copy.22
  357.1 1.3 copy.21
Async XLA Ops:
  7.2 1.6 copy-start
  7.2 99.1 %reduce-scatter.2.cloned.1.call-start = ((), (), s32[]{:S(2)}) async-start(), calls=%async_computation.1 | async-start | bytes 4718592 | tf_op jit(solution)/shard_map/reduce_scatter | solution.py:34
  14.6 0.9 copy-start.6
  14.7 93.2 %copy-start.2 = (f32[512,512]{1,0:T(8,128)S(1)}, f32[512,512]{1,0:T(8,128)}, u32[]{:S(2)}) copy-start(f32[512,512]{1,0:T(8,128)} %param.16) | copy-start | bytes 3145732
  14.7 205.1 %all-reduce.5.cloned.1.call-start = ((), (), s32[]{:S(2)}) async-start(), calls=%async_computation.2 | async-start | bytes 4194304 | tf_op jit(solution)/shard_map/psum | solution.py:53
  106.2 4.5 %copy-start.3 = (f32[128,1024]{0,1:T(8,128)S(1)}, f32[128,1024]{0,1:T(8,128)}, u32[]{:S(2)}) copy-start(f32[128,1024]{0,1:T(8,128)} %reduce-scatter.2.cloned.1.call-done) | copy-start | bytes 1572868
  107.8 3.6 copy-start.5
  111.5 1.8 copy-start.4
  111.5 3.3 copy-start.1
  117.7 223.6 %all-reduce.7.cloned.1.call-start = ((), (), s32[]{:S(2)}) async-start(), calls=%async_computation.3 | async-start | bytes 12582912 | tf_op jit(solution)/shard_map/psum | solution.py:40
Sparse Core Ops, SparseCore 0:
  14.8 91.4 reduce-scatter.1
  117.8 101.9 all-reduce.4
  222.3 118.8 all-reduce.6
